TPU v7x, 32 devices: a whole 2x2x4 slice. The times are simulated.
32 devices in a mesh: dp: 8 (over z, x), row: 2 (over y), col: 2 (over core).
Axes of the slice: x: 2, y: 2, z: 4, core: 2. Of those that a mesh axis runs over, the one named last changes fastest.
Arguments:
- block_in: float32 [8192, 768], P(('dp', 'row'), 'col'), may hold values from -6 to 6
- upstream: float32 [8192, 768], P(('dp', 'row'), 'col'), may hold values from -6 to 6
- norm_params: float32 [4, 768], P(None, 'col'), may hold values from -0.5 to 1.5
- w_qkv: float32 [3, 12, 64, 768], P(None, 'row', 'dp', 'col'), may hold values from -1.4433757 to 1.4433757
- w_attn: float32 [12, 64, 768], P('row', 'dp', 'col'), may hold values from -0.875 to 0.875
- w_up: float32 [3072, 768], P(('dp', 'row'), 'col'), may hold values from -0.21875 to 0.21875
- w_down: float32 [3072, 768], P(('dp', 'row'), 'col'), may hold values from -0.109375 to 0.109375
- mom_norm: float32 [2, 4, 768], P(None, None, 'col'), may hold values from -0.224 to 0.224, as said below
- mom_qkv: float32 [2, 3, 12, 64, 768], P(None, None, 'row', 'dp', 'col'), may hold values from -0.16 to 0.16, as said below
- mom_attn: float32 [2, 12, 64, 768], P(None, 'row', 'dp', 'col'), may hold values from -0.048 to 0.048, as said below
- mom_up: float32 [2, 3072, 768], P(None, ('dp', 'row'), 'col'), may hold values from -0.128 to 0.128, as said below
- mom_down: float32 [2, 3072, 768], P(None, ('dp', 'row'), 'col'), may hold values from -0.208 to 0.208, as said below
Outputs:
- block_out: float32 [8192, 768], P(('dp', 'row'), 'col')
- input_grad: float32 [8192, 768], P(('dp', 'row'), 'col')
- grad_norm: float32 [4, 768], P(None, 'col')
- grad_qkv: float32 [3, 12, 64, 768], P(None, 'row', 'dp', 'col')
- grad_attn: float32 [12, 64, 768], P('row', 'dp', 'col')
- grad_up: float32 [3072, 768], P(('dp', 'row'), 'col')
- grad_down: float32 [3072, 768], P(('dp', 'row'), 'col')
- new_norm: float32 [4, 768], P(None, 'col')
- new_qkv: float32 [3, 12, 64, 768], P(None, 'row', 'dp', 'col')
- new_attn: float32 [12, 64, 768], P('row', 'dp', 'col')
- new_up: float32 [3072, 768], P(('dp', 'row'), 'col')
- new_down: float32 [3072, 768], P(('dp', 'row'), 'col')
- new_mom_norm: float32 [2, 4, 768], P(None, None, 'col')
- new_mom_qkv: float32 [2, 3, 12, 64, 768], P(None, None, 'row', 'dp', 'col')
- new_mom_attn: float32 [2, 12, 64, 768], P(None, 'row', 'dp', 'col')
- new_mom_up: float32 [2, 3072, 768], P(None, ('dp', 'row'), 'col')
- new_mom_down: float32 [2, 3072, 768], P(None, ('dp', 'row'), 'col')
Inputs may be any that keep to these rules, and one draw needn't show every extreme that they name: `mom_norm`: second moments are positive. `mom_qkv`: second moments are positive. `mom_attn`: second moments are positive. `mom_up`: second moments are positive. `mom_down`: second moments are positive.
All inputs are finite; a program needn't handle non-finite values.
Results may differ from a plain program's by a relative error of at most 0.012.
The roundings to bfloat16 on the way count: a program that leaves them out, or rounds other values in their place, can miss the bound.
Values may be sent and summed in bfloat16 or wider, within the bound.
A program may use at most 128 MiB of HBM per device.

v0:
```python
import math
import jax
import jax.numpy as jnp
from jax import lax
from jax.sharding import PartitionSpec as P

SEQ = 512
STEP = 4
norm_eps = 1e-05
adam_eps = 1e-08
beta_one = 0.9
beta_two = 0.95
learn_rate = 0.02
decay_rate = 0.1
gelu_coef = math.sqrt(2.0 / math.pi)
cubic_coef = 0.044715
masked_score = -1e30


def smooth_pair(values):
    squared = values * values
    bent = jnp.tanh(gelu_coef * (values + cubic_coef * squared * values))
    smooth = 0.5 * values * (1.0 + bent)
    slope = 0.5 * (1.0 + bent) + 0.5 * values * (1.0 - bent * bent) * gelu_coef * (
        1.0 + 3.0 * cubic_coef * squared
    )
    return (smooth, slope)


def feature_total(pieces):
    return lax.psum(pieces, "col")


def normalize(rows_in, gain_row, shift_row):
    feature_count = rows_in.shape[1] * lax.axis_size("col")
    (row_total,) = feature_total((jnp.sum(rows_in, axis=1, keepdims=True),))
    center = rows_in - row_total / feature_count
    (square_total,) = feature_total((jnp.sum(center * center, axis=1, keepdims=True),))
    spread = square_total / feature_count
    inverse = lax.rsqrt(spread + norm_eps)
    normal = center * inverse
    return (normal, inverse, (normal * gain_row + shift_row).astype(jnp.bfloat16))


def norm_back(grad_normed, normal, inverse, gain_row):
    feature_count = grad_normed.shape[1] * lax.axis_size("col")
    scaled = grad_normed * gain_row
    first_total, second_total = feature_total(
        (jnp.sum(scaled, axis=1, keepdims=True), jnp.sum(scaled * normal, axis=1, keepdims=True))
    )
    return inverse * (
        scaled - first_total / feature_count - normal * (second_total / feature_count)
    )


def rows_then_cols(local_rows, weight):
    everyone = lax.all_gather(local_rows, "row", axis=0, tiled=True)
    return (
        lax.psum_scatter(
            lax.dot_general(
                everyone, weight, (((1,), (1,)), ((), ())), preferred_element_type=jnp.float32
            ),
            "col",
            scatter_dimension=0,
            tiled=True,
        ),
        everyone,
    )


def cols_then_rows(local_rows, weight):
    everyone = lax.all_gather(local_rows, "col", axis=0, tiled=True)
    return (
        lax.psum_scatter(
            jnp.dot(everyone, weight, preferred_element_type=jnp.float32),
            "row",
            scatter_dimension=0,
            tiled=True,
        ),
        everyone,
    )


def token_product(left_rows, right_rows):
    return lax.dot_general(
        left_rows, right_rows, (((0,), (0,)), ((), ())), preferred_element_type=jnp.float32
    )


def causal_mask(length):
    return lax.broadcasted_iota(jnp.int32, (length, length), 0) >= lax.broadcasted_iota(
        jnp.int32, (length, length), 1
    )


def seq_scores(qkv_seq):
    score_scale = 1.0 / math.sqrt(qkv_seq.shape[3])
    scores = (
        jnp.einsum("qhd,khd->hqk", qkv_seq[:, 0], qkv_seq[:, 1], preferred_element_type=jnp.float32)
        * score_scale
    )
    return (jnp.where(causal_mask(qkv_seq.shape[0])[None], scores, masked_score), score_scale)


def attend(qkv_seq):
    scores, score_scale = seq_scores(qkv_seq)
    highest = jnp.max(scores, axis=2, keepdims=True)
    log_total = highest + jnp.log(jnp.sum(jnp.exp(scores - highest), axis=2, keepdims=True))
    attn_probs = jnp.exp(scores - log_total).astype(jnp.bfloat16)
    mixed = jnp.einsum(
        "hqk,khd->qhd", attn_probs, qkv_seq[:, 2], preferred_element_type=jnp.float32
    )
    return (mixed.astype(jnp.bfloat16).reshape(qkv_seq.shape[0], -1), log_total)


def attend_back(operands):
    qkv_seq, grad_mixed, log_total = operands
    grad_mixed = grad_mixed.reshape(qkv_seq.shape[0], qkv_seq.shape[2], qkv_seq.shape[3])
    scores, score_scale = seq_scores(qkv_seq)
    attn_probs = jnp.exp(scores - log_total)
    grad_values = jnp.einsum(
        "hqk,qhd->khd",
        attn_probs.astype(jnp.bfloat16),
        grad_mixed,
        preferred_element_type=jnp.float32,
    )
    grad_probs = jnp.einsum(
        "qhd,khd->hqk", grad_mixed, qkv_seq[:, 2], preferred_element_type=jnp.float32
    )
    delta_rows = jnp.sum(attn_probs * grad_probs, axis=2, keepdims=True)
    grad_scores = (attn_probs * (grad_probs - delta_rows) * score_scale).astype(jnp.bfloat16)
    grad_queries = jnp.einsum(
        "hqk,khd->qhd", grad_scores, qkv_seq[:, 1], preferred_element_type=jnp.float32
    )
    grad_keys = jnp.einsum(
        "hqk,qhd->khd", grad_scores, qkv_seq[:, 0], preferred_element_type=jnp.float32
    )
    return jnp.stack([grad_queries, grad_keys, grad_values], axis=1).astype(jnp.bfloat16)


def adam_step(weight, grad, moments, decay):
    first_moment = beta_one * moments[0] + (1.0 - beta_one) * grad
    second_moment = beta_two * moments[1] + (1.0 - beta_two) * grad * grad
    step_size = (
        first_moment
        / (1.0 - beta_one**STEP)
        / (jnp.sqrt(second_moment / (1.0 - beta_two**STEP)) + adam_eps)
    )
    return (
        weight - learn_rate * (step_size + decay * weight),
        jnp.stack([first_moment, second_moment]),
    )


def on_device(
    block_in,
    upstream,
    norm_params,
    w_qkv,
    w_attn,
    w_up,
    w_down,
    mom_norm,
    mom_qkv,
    mom_attn,
    mom_up,
    mom_down,
):
    qkv_block, attn_block, up_block, down_block = (
        lax.all_gather(w_qkv.astype(jnp.bfloat16), "dp", axis=2, tiled=True),
        lax.all_gather(w_attn.astype(jnp.bfloat16), "dp", axis=1, tiled=True),
        lax.all_gather(w_up.astype(jnp.bfloat16), "dp", axis=0, tiled=True),
        lax.all_gather(w_down.astype(jnp.bfloat16), "dp", axis=0, tiled=True),
    )
    heads_here = qkv_block.shape[1]
    head_size = qkv_block.shape[2]
    feature_here = qkv_block.shape[3]
    qkv_mat = qkv_block.reshape(3 * heads_here * head_size, feature_here)
    attn_mat = attn_block.reshape(heads_here * head_size, feature_here)
    normal_one, inverse_one, normed_one = normalize(block_in, norm_params[0], norm_params[1])
    triples, normed_one_all = rows_then_cols(normed_one, qkv_mat)
    triples = triples.astype(jnp.bfloat16).reshape(-1, SEQ, 3, heads_here, head_size)
    mixed, log_total = lax.map(attend, triples)
    mixed = mixed.reshape(-1, heads_here * head_size)
    attn_branch, mixed_all = cols_then_rows(mixed, attn_mat)
    middle = block_in + attn_branch
    normal_two, inverse_two, normed_two = normalize(middle, norm_params[2], norm_params[3])
    hidden_pre, normed_two_all = rows_then_cols(normed_two, up_block)
    activated, slope = smooth_pair(hidden_pre)
    activated = activated.astype(jnp.bfloat16)
    mlp_branch, activated_all = cols_then_rows(activated, down_block)
    block_out = middle + mlp_branch
    upstream_b = upstream.astype(jnp.bfloat16)
    grad_hidden, upstream_all = rows_then_cols(upstream_b, down_block)
    grad_down = token_product(activated_all, upstream_all)
    grad_pre = (grad_hidden * slope).astype(jnp.bfloat16)
    grad_normed_two, grad_pre_all = cols_then_rows(grad_pre, up_block)
    grad_up = token_product(grad_pre_all, normed_two_all)
    middle_grad = upstream + norm_back(grad_normed_two, normal_two, inverse_two, norm_params[2])
    middle_b = middle_grad.astype(jnp.bfloat16)
    grad_mixed, middle_all = rows_then_cols(middle_b, attn_mat)
    grad_attn = token_product(mixed_all, middle_all).reshape(heads_here, head_size, feature_here)
    grad_mixed = grad_mixed.astype(jnp.bfloat16).reshape(
        triples.shape[0], SEQ, heads_here * head_size
    )
    grad_triples = lax.map(attend_back, (triples, grad_mixed, log_total))
    grad_triples = grad_triples.reshape(-1, 3 * heads_here * head_size)
    grad_normed_one, triples_all = cols_then_rows(grad_triples, qkv_mat)
    grad_qkv = token_product(triples_all, normed_one_all).reshape(
        3, heads_here, head_size, feature_here
    )
    input_grad = middle_grad + norm_back(grad_normed_one, normal_one, inverse_one, norm_params[0])
    norm_terms = jnp.stack(
        [
            jnp.sum(grad_normed_one * normal_one, axis=0),
            jnp.sum(grad_normed_one, axis=0),
            jnp.sum(grad_normed_two * normal_two, axis=0),
            jnp.sum(grad_normed_two, axis=0),
        ]
    )
    (grad_norm,) = lax.psum((norm_terms,), ("dp", "row"))
    grad_qkv, grad_attn, grad_up, grad_down = (
        lax.psum_scatter(grad_qkv, "dp", scatter_dimension=2, tiled=True),
        lax.psum_scatter(grad_attn, "dp", scatter_dimension=1, tiled=True),
        lax.psum_scatter(grad_up, "dp", scatter_dimension=0, tiled=True),
        lax.psum_scatter(grad_down, "dp", scatter_dimension=0, tiled=True),
    )
    token_count = block_in.shape[0] * lax.axis_size("dp") * lax.axis_size("row")
    factor = 1.0 / math.sqrt(token_count)
    grad_norm = grad_norm * factor
    grad_qkv = grad_qkv * factor
    grad_attn = grad_attn * factor
    grad_up = grad_up * factor
    grad_down = grad_down * factor
    new_norm, new_mom_norm = adam_step(norm_params, grad_norm, mom_norm, 0.0)
    new_qkv, new_mom_qkv = adam_step(w_qkv, grad_qkv, mom_qkv, decay_rate)
    new_attn, new_mom_attn = adam_step(w_attn, grad_attn, mom_attn, decay_rate)
    new_up, new_mom_up = adam_step(w_up, grad_up, mom_up, decay_rate)
    new_down, new_mom_down = adam_step(w_down, grad_down, mom_down, decay_rate)
    return (
        block_out,
        input_grad,
        grad_norm,
        grad_qkv,
        grad_attn,
        grad_up,
        grad_down,
        new_norm,
        new_qkv,
        new_attn,
        new_up,
        new_down,
        new_mom_norm,
        new_mom_qkv,
        new_mom_attn,
        new_mom_up,
        new_mom_down,
    )


def solution(mesh):
    in_specs = (
        P(("dp", "row"), "col"),
        P(("dp", "row"), "col"),
        P(None, "col"),
        P(None, "row", "dp", "col"),
        P("row", "dp", "col"),
        P(("dp", "row"), "col"),
        P(("dp", "row"), "col"),
        P(None, None, "col"),
        P(None, None, "row", "dp", "col"),
        P(None, "row", "dp", "col"),
        P(None, ("dp", "row"), "col"),
        P(None, ("dp", "row"), "col"),
    )
    out_specs = (
        P(("dp", "row"), "col"),
        P(("dp", "row"), "col"),
        P(None, "col"),
        P(None, "row", "dp", "col"),
        P("row", "dp", "col"),
        P(("dp", "row"), "col"),
        P(("dp", "row"), "col"),
        P(None, "col"),
        P(None, "row", "dp", "col"),
        P("row", "dp", "col"),
        P(("dp", "row"), "col"),
        P(("dp", "row"), "col"),
        P(None, None, "col"),
        P(None, None, "row", "dp", "col"),
        P(None, "row", "dp", "col"),
        P(None, ("dp", "row"), "col"),
        P(None, ("dp", "row"), "col"),
    )
    return jax.shard_map(
        on_device, mesh=mesh, in_specs=in_specs, out_specs=out_specs, check_vma=False
    )
```

profile of v0, /device:TPU:0, one launch (start us, length us, event | category | flops | bytes accessed | tf_op | source)
XLA Modules:
  0.0 679.9 jit_solution(14349840694385199696)
XLA Ops:
  19.0 13.0 %all_gather.36 = bf16[1024,384]{1,0:T(8,128)(2,1)S(1)} all-gather(bf16[512,384]{1,0:T(8,128)(2,1)S(1)} %add_convert_fusion.1), channel_id=1, replica_groups=mesh['dp'=8,'row'=2,'col'=2] {'row'}, dimensions={0}, use_global_device_ids=true | all-gather | bytes 1179648 | tf_op jit(solution)/shard_map/all_gather | solution.py:57
  32.0 33.5 %all_gather.37 = bf16[3,6,64,384]{3,2,1,0:T(8,128)(2,1)S(1)} all-gather(bf16[3,6,8,384]{3,2,1,0:T(8,128)(2,1)S(1)} %convert_element_type.60), channel_id=1, replica_groups=mesh['dp'=8,'row'=2,'col'=2] {'dp'}, dimensions={2}, use_global_device_ids=true | all-gather | bytes 995328 | tf_op jit(solution)/shard_map/all_gather | solution.py:170
  71.9 31.2 %all_gather.39 = bf16[6,64,384]{2,1,0:T(8,128)(2,1)S(1)} all-gather(bf16[6,8,384]{2,1,0:T(8,128)(2,1)S(1)} %convert_element_type.65), channel_id=1, replica_groups=mesh['dp'=8,'row'=2,'col'=2] {'dp'}, dimensions={1}, use_global_device_ids=true | all-gather | bytes 331776 | tf_op jit(solution)/shard_map/all_gather | solution.py:171
  119.5 17.4 %all_gather.44 = bf16[1024,384]{1,0:T(8,128)(2,1)S(1)} all-gather(bf16[512,384]{1,0:T(8,128)(2,1)S(1)} %convert_element_type.70), channel_id=1, replica_groups=mesh['dp'=8,'row'=2,'col'=2] {'row'}, dimensions={0}, use_global_device_ids=true | all-gather | bytes 1179648 | tf_op jit(solution)/shard_map/all_gather | solution.py:57
  136.8 6.0 fusion.73
  143.0 6.5 reduce-scatter.15.cloned.1.call-done
  156.2 24.1 %all_gather.40 = bf16[1024,384]{1,0:T(8,128)(2,1)} all-gather(bf16[512,384]{1,0:T(8,128)(2,1)S(1)} %add_convert_fusion), channel_id=1, replica_groups=mesh['dp'=8,'row'=2,'col'=2] {'row'}, dimensions={0}, use_global_device_ids=true | all-gather | bytes 1179648 | tf_op jit(solution)/shard_map/all_gather | solution.py:57
  180.3 5.9 fusion.71
  186.3 14.2 %reduce-scatter.17.cloned.1.call-done = f32[512,1536]{1,0:T(8,128)} async-done(((f32[1024,1536]{1,0:T(8,128)}), f32[512,1536]{1,0:T(8,128)}) %reduce-scatter.17.cloned.1.call-update) | async-done | bytes 3145744 | tf_op jit(solution)/shard_map/reduce_scatter | solution.py:59
  200.5 5.2 multiply_convert_fusion.1
  206.3 13.7 %all-gather.12.cloned.1.call-done = bf16[1024,1536]{1,0:T(8,128)(2,1)} async-done(((bf16[512,1536]{1,0:T(8,128)(2,1)}), bf16[1024,1536]{1,0:T(8,128)(2,1)}) %all-gather.12.cloned.1.call-update) | async-done | bytes 3145744 | tf_op jit(solution)/shard_map/all_gather | solution.py:72
  220.0 5.2 fusion.74
  225.3 9.4 %all-gather.8.cloned.1.call-done = bf16[1024,1536]{1,0:T(8,128)(2,1)} async-done(((bf16[512,1536]{1,0:T(8,128)(2,1)}), bf16[1024,1536]{1,0:T(8,128)(2,1)}) %all-gather.8.cloned.1.call-update) | async-done | bytes 3145744 | tf_op jit(solution)/shard_map/all_gather | solution.py:72
  234.7 5.1 fusion.72
  240.0 24.4 %reduce-scatter.23.cloned.1.call-done = f32[512,384]{1,0:T(8,128)} async-done(((f32[1024,384]{1,0:T(8,128)}), f32[512,384]{1,0:T(8,128)}) %reduce-scatter.23.cloned.1.call-update) | async-done | bytes 786448 | tf_op jit(solution)/shard_map/reduce_scatter | solution.py:74
  268.9 23.8 %reduce-scatter.19.cloned.1.call-done = f32[512,384]{1,0:T(8,128)} async-done(((f32[1024,384]{1,0:T(8,128)}), f32[512,384]{1,0:T(8,128)}) %reduce-scatter.19.cloned.1.call-update) | async-done | bytes 786448 | tf_op jit(solution)/shard_map/reduce_scatter | solution.py:74
  295.8 11.3 %all_gather.46 = bf16[1024,384]{1,0:T(8,128)(2,1)S(1)} all-gather(bf16[512,384]{1,0:T(8,128)(2,1)S(1)} %get-tuple-element.70), channel_id=1, replica_groups=mesh['dp'=8,'row'=2,'col'=2] {'row'}, dimensions={0}, use_global_device_ids=true | all-gather | bytes 1179648 | tf_op jit(solution)/shard_map/all_gather | solution.py:57
  309.0 9.1 %reduce-scatter.25.cloned.1.call-done = f32[512,384]{1,0:T(8,128)} async-done(((f32[1024,384]{1,0:T(8,128)}), f32[512,384]{1,0:T(8,128)}) %reduce-scatter.25.cloned.1.call-update) | async-done | bytes 786448 | tf_op jit(solution)/shard_map/reduce_scatter | solution.py:59
  321.2 5.2 fusion.36
  326.4 4.7 fusion.43
  331.1 13.3 %fusion.40 = bf16[512,1,6,64]{0,3,2,1:T(8,128)(2,1)} fusion(f32[6,512,512]{1,2,0:T(8,128)} %fusion.43, f32[6,512,512]{1,2,0:T(8,128)} %copy-done.1, f32[6,512]{1,0:T(8,128)} %copy-done.28, pred[512,512]{0,1:T(8,128)(4,1)} %copy-done.17, bf16[512,3,6,64]{0,3,2,1:T(8,128)(2,1)} %bitcast.169), kind=kOutput, calls=%fused_computation.30 | convolution fusion | flops 218828288 | bytes 26509312 | tf_op jit(solution)/shard_map/while/body/eval_jaxpr/hqk,khd->qhd/dot_general | solution.py:132
  344.4 13.4 %fusion.37 = bf16[512,1,6,64]{0,3,2,1:T(8,128)(2,1)} fusion(f32[6,512,512]{1,2,0:T(8,128)} %fusion.43, f32[6,512,512]{1,2,0:T(8,128)} %copy-done.1, f32[6,512]{1,0:T(8,128)} %copy-done.28, pred[512,512]{0,1:T(8,128)(4,1)} %copy-done.17, bf16[512,3,6,64]{0,3,2,1:T(8,128)(2,1)} %bitcast.170), kind=kOutput, calls=%fused_computation.29 | convolution fusion | flops 218828288 | bytes 26509312 | tf_op jit(solution)/shard_map/while/body/eval_jaxpr/hqk,qhd->khd/dot_general | solution.py:135
  361.8 5.3 fusion.79
  367.2 5.6 fusion.80
  372.9 4.4 fusion.76
  377.4 4.4 fusion.77
  381.8 44.2 %reduce-scatter.31.cloned.1.call-done = f32[6,8,384]{2,1,0:T(8,128)} async-done(((f32[6,64,384]{2,1,0:T(8,128)}), f32[6,8,384]{2,1,0:T(8,128)}) %reduce-scatter.31.cloned.1.call-update) | async-done | bytes 73744 | tf_op jit(solution)/shard_map/reduce_scatter | solution.py:224
  429.2 69.5 %reduce-scatter.33.cloned.1.call-done = f32[192,384]{1,0:T(8,128)} async-done(((f32[1536,384]{1,0:T(8,128)}), f32[192,384]{1,0:T(8,128)}) %reduce-scatter.33.cloned.1.call-update) | async-done | bytes 294928 | tf_op jit(solution)/shard_map/reduce_scatter | solution.py:225
  500.7 70.5 %reduce-scatter.35.cloned.1.call-done = f32[192,384]{1,0:T(8,128)} async-done(((f32[1536,384]{1,0:T(8,128)}), f32[192,384]{1,0:T(8,128)}) %reduce-scatter.35.cloned.1.call-update) | async-done | bytes 294928 | tf_op jit(solution)/shard_map/reduce_scatter | solution.py:226
  577.1 21.6 %reduce-scatter.27.cloned.1.call-done = f32[512,384]{1,0:T(8,128)} async-done(((f32[1024,384]{1,0:T(8,128)}), f32[512,384]{1,0:T(8,128)}) %reduce-scatter.27.cloned.1.call-update) | async-done | bytes 786448 | tf_op jit(solution)/shard_map/reduce_scatter | solution.py:74
  603.0 41.8 %psum.71 = f32[4,384]{1,0:T(4,128)S(1)} all-reduce(f32[4,384]{1,0:T(4,128)S(1)} %pad_maximum_fusion.6), channel_id=1, replica_groups=mesh['dp'=8,'row'=2,'col'=2] {'dp','row'}, use_global_device_ids=true, to_apply=%region_31.32 | all-reduce | flops 1536 | bytes 12288 | tf_op jit(solution)/shard_map/psum | solution.py:221
  648.5 19.9 %reduce-scatter.29.cloned.1.call-done = f32[3,6,8,384]{3,2,1,0:T(8,128)} async-done(((f32[3,6,64,384]{3,2,1,0:T(8,128)}), f32[3,6,8,384]{3,2,1,0:T(8,128)}) %reduce-scatter.29.cloned.1.call-update) | async-done | bytes 221200 | tf_op jit(solution)/shard_map/reduce_scatter | solution.py:223
  (163 shorter events, 80.4 us)
Async XLA Ops:
  8.0 95.0 %reduce-scatter.13.cloned.1.call-start = ((), (), s32[]{:S(2)}) async-start(), calls=%async_computation.12 | async-start | bytes 7077888 | tf_op jit(solution)/shard_map/reduce_scatter | solution.py:59
  70.1 66.8 %all-gather.10.cloned.1.call-start = ((), (), s32[]{:S(2)}) async-start(), calls=%async_computation.17 | async-start | bytes 1327104 | tf_op jit(solution)/shard_map/all_gather | solution.py:173
  71.7 77.8 %reduce-scatter.15.cloned.1.call-start = ((), (), s32[]{:S(2)}) async-start(), calls=%async_computation.13 | async-start | bytes 2359296 | tf_op jit(solution)/shard_map/reduce_scatter | solution.py:74
  71.8 38.2 %copy-start.17 = (pred[512,512]{0,1:T(8,128)(4,1)}, pred[512,512]{0,1:T(8,128)(4,1)S(1)}, u32[]{:S(2)}) copy-start(pred[512,512]{0,1:T(8,128)(4,1)S(1)} %iota_compare_fusion) | copy-start | bytes 786436
  118.6 61.7 %all-gather.6.cloned.1.call-start = ((), (), s32[]{:S(2)}) async-start(), calls=%async_computation.14 | async-start | bytes 1327104 | tf_op jit(solution)/shard_map/all_gather | solution.py:172
  119.3 67.0 %reduce-scatter.21.cloned.1.call-start = ((), (), s32[]{:S(2)}) async-start(), calls=%async_computation.19 | async-start | bytes 9437184 | tf_op jit(solution)/shard_map/reduce_scatter | solution.py:59
  142.9 57.6 %reduce-scatter.17.cloned.1.call-start = ((), (), s32[]{:S(2)}) async-start(), calls=%async_computation.15 | async-start | bytes 9437184 | tf_op jit(solution)/shard_map/reduce_scatter | solution.py:59
  186.3 33.8 %all-gather.12.cloned.1.call-start = ((), (), s32[]{:S(2)}) async-start(), calls=%async_computation.20 | async-start | bytes 4718592 | tf_op jit(solution)/shard_map/all_gather | solution.py:72
  205.7 29.0 %all-gather.8.cloned.1.call-start = ((), (), s32[]{:S(2)}) async-start(), calls=%async_computation.16 | async-start | bytes 4718592 | tf_op jit(solution)/shard_map/all_gather | solution.py:72
  206.3 58.1 %reduce-scatter.23.cloned.1.call-start = ((), (), s32[]{:S(2)}) async-start(), calls=%async_computation.21 | async-start | bytes 2359296 | tf_op jit(solution)/shard_map/reduce_scatter | solution.py:74
  225.3 67.5 %reduce-scatter.19.cloned.1.call-start = ((), (), s32[]{:S(2)}) async-start(), calls=%async_computation.18 | async-start | bytes 2359296 | tf_op jit(solution)/shard_map/reduce_scatter | solution.py:74
  239.9 78.2 %reduce-scatter.25.cloned.1.call-start = ((), (), s32[]{:S(2)}) async-start(), calls=%async_computation.22 | async-start | bytes 2359296 | tf_op jit(solution)/shard_map/reduce_scatter | solution.py:59
  308.9 63.9 %all-gather.14.cloned.1.call-start = ((), (), s32[]{:S(2)}) async-start(), calls=%async_computation.23 | async-start | bytes 3538944 | tf_op jit(solution)/shard_map/all_gather | solution.py:72
  344.4 13.4 %copy-start.21 = (bf16[512,1,6,64]{0,3,2,1:T(8,128)(2,1)S(1)}, bf16[512,1,6,64]{0,3,2,1:T(8,128)(2,1)}, u32[]{:S(2)}) copy-start(bf16[512,1,6,64]{0,3,2,1:T(8,128)(2,1)} %fusion.36) | copy-start | bytes 1179652
  360.0 65.9 %reduce-scatter.31.cloned.1.call-start = ((), (), s32[]{:S(2)}) async-start(), calls=%async_computation.26 | async-start | bytes 663552 | tf_op jit(solution)/shard_map/reduce_scatter | solution.py:224
  361.5 137.2 %reduce-scatter.33.cloned.1.call-start = ((), (), s32[]{:S(2)}) async-start(), calls=%async_computation.27 | async-start | bytes 2654208 | tf_op jit(solution)/shard_map/reduce_scatter | solution.py:225
  367.1 204.1 %reduce-scatter.35.cloned.1.call-start = ((), (), s32[]{:S(2)}) async-start(), calls=%async_computation.28 | async-start | bytes 2654208 | tf_op jit(solution)/shard_map/reduce_scatter | solution.py:226
  372.8 226.0 %reduce-scatter.27.cloned.1.call-start = ((), (), s32[]{:S(2)}) async-start(), calls=%async_computation.24 | async-start | bytes 2359296 | tf_op jit(solution)/shard_map/reduce_scatter | solution.py:74
  377.3 48.7 %copy-start.20 = (f32[2,6,8,384]{3,2,1,0:T(8,128)S(1)}, f32[2,6,8,384]{3,2,1,0:T(8,128)}, u32[]{:S(2)}) copy-start(f32[2,6,8,384]{3,2,1,0:T(8,128)} %param.21) | copy-start | bytes 442372
  377.3 50.3 %copy-start.24 = (f32[6,8,384]{2,1,0:T(8,128)S(1)}, f32[6,8,384]{2,1,0:T(8,128)}, u32[]{:S(2)}) copy-start(f32[6,8,384]{2,1,0:T(8,128)} %param.16) | copy-start | bytes 221188
  377.3 291.1 %reduce-scatter.29.cloned.1.call-start = ((), (), s32[]{:S(2)}) async-start(), calls=%async_computation.25 | async-start | bytes 1990656 | tf_op jit(solution)/shard_map/reduce_scatter | solution.py:223
  381.7 117.0 %copy-start.8 = (f32[2,192,384]{2,1,0:T(8,128)S(1)}, f32[2,192,384]{2,1,0:T(8,128)}, u32[]{:S(2)}) copy-start(f32[2,192,384]{2,1,0:T(8,128)} %param.22) | copy-start | bytes 1769476
  381.7 189.4 %copy-start.9 = (f32[2,192,384]{2,1,0:T(8,128)S(1)}, f32[2,192,384]{2,1,0:T(8,128)}, u32[]{:S(2)}) copy-start(f32[2,192,384]{2,1,0:T(8,128)} %param.23) | copy-start | bytes 1769476
  426.9 146.3 %copy-start.22 = (f32[6,8,384]{2,1,0:T(8,128)}, f32[6,8,384]{2,1,0:T(8,128)S(1)}, u32[]{:S(2)}) copy-start(f32[6,8,384]{2,1,0:T(8,128)S(1)} %get-tuple-element.65) | copy-start | bytes 221188
  499.8 77.4 %copy-start.11 = (f32[192,384]{1,0:T(8,128)}, f32[192,384]{1,0:T(8,128)S(1)}, u32[]{:S(2)}) copy-start(f32[192,384]{1,0:T(8,128)S(1)} %get-tuple-element.63) | copy-start | bytes 884740
  572.3 28.0 %copy-start.12 = (f32[192,384]{1,0:T(8,128)}, f32[192,384]{1,0:T(8,128)S(1)}, u32[]{:S(2)}) copy-start(f32[192,384]{1,0:T(8,128)S(1)} %get-tuple-element.61) | copy-start | bytes 884740
  572.3 72.5 %copy-start.25 = (f32[2,4,384]{2,1,0:T(4,128)S(1)}, f32[2,4,384]{2,1,0:T(4,128)}, u32[]{:S(2)}) copy-start(f32[2,4,384]{2,1,0:T(4,128)} %param.19) | copy-start | bytes 36868
  572.4 73.1 %copy-start.26 = (f32[4,384]{1,0:T(4,128)S(1)}, f32[4,384]{1,0:T(4,128)}, u32[]{:S(2)}) copy-start(f32[4,384]{1,0:T(4,128)} %param.14) | copy-start | bytes 18436
  572.4 73.8 %copy-start.7 = (f32[512,384]{1,0:T(8,128)S(1)}, f32[512,384]{1,0:T(8,128)}, u32[]{:S(2)}) copy-start(f32[512,384]{1,0:T(8,128)} %get-tuple-element.71) | copy-start | bytes 2359300
  575.2 93.2 %copy-start.10 = (f32[2,3,6,8,384]{4,3,2,1,0:T(8,128)S(1)}, f32[2,3,6,8,384]{4,3,2,1,0:T(8,128)}, u32[]{:S(2)}) copy-start(f32[2,3,6,8,384]{4,3,2,1,0:T(8,128)} %param.20) | copy-start | bytes 1327108
  600.3 69.9 %copy-start.18 = (f32[3,6,8,384]{3,2,1,0:T(8,128)S(1)}, f32[3,6,8,384]{3,2,1,0:T(8,128)}, u32[]{:S(2)}) copy-start(f32[3,6,8,384]{3,2,1,0:T(8,128)} %param.15) | copy-start | bytes 663556
  644.9 27.2 %copy-start.27 = (f32[4,384]{1,0:T(4,128)}, f32[4,384]{1,0:T(4,128)S(1)}, u32[]{:S(2)}) copy-start(f32[4,384]{1,0:T(4,128)S(1)} %get-tuple-element.69) | copy-start | bytes 18436
  (15 other events, 56.1 us)
Sparse Core Ops, SparseCore 0:
  70.2 12.6 reduce-scatter.12
  118.7 30.7 reduce-scatter.14
  151.8 14.0 reduce-scatter.20
  186.4 14.0 reduce-scatter.16
  205.8 14.1 all-gather.11
  221.4 13.2 all-gather.7
  237.0 27.3 reduce-scatter.22
  266.6 26.1 reduce-scatter.18
  309.1 9.0 reduce-scatter.24
  360.2 12.2 all-gather.13
Sparse Core Ops, SparseCore 1:
  73.3 41.7 all-gather.9
  121.8 41.2 all-gather.5
  364.4 61.5 reduce-scatter.30
  429.5 69.1 reduce-scatter.32
  502.2 68.9 reduce-scatter.34
  573.5 25.3 reduce-scatter.26
  602.1 66.2 reduce-scatter.28
where the time goes:
time: 689 us; the launch traced here: 680 us
  waiting for transfers between devices  328 us (48%)
  blocking collectives  190 us (28%)
  matrix products  92.3 us (13%)
  other arithmetic  45.7 us (7%)
  between operations  16.5 us (2%)
    reduce_scatter x4, waiting for transfers between devices, cols_then_rows(): lax.psum_scatter(jnp.dot(everyone, weight, preferred_element_type=jnp.flo...  76.4 us
    reduce_scatter x1, waiting for transfers between devices, on_device(): lax.psum_scatter(grad_down, 'dp', scatter_dimension=0, tiled=True)  70.5 us
    reduce_scatter x1, waiting for transfers between devices, on_device(): lax.psum_scatter(grad_up, 'dp', scatter_dimension=0, tiled=True)  69.5 us
    all_gather x4, blocking collectives, rows_then_cols(): everyone = lax.all_gather(local_rows, 'row', axis=0, tiled=True)  65.7 us
    reduce_scatter x1, waiting for transfers between devices, on_device(): lax.psum_scatter(grad_attn, 'dp', scatter_dimension=1, tiled=True)  44.2 us
    psum x1, blocking collectives, on_device(): grad_norm, = lax.psum((norm_terms,), ('dp', 'row'))  41.8 us
    all_gather x1, blocking collectives, on_device(): lax.all_gather(w_qkv.astype(jnp.bfloat16), 'dp', axis=2, tiled=True)  33.5 us
    all_gather x1, blocking collectives, on_device(): lax.all_gather(w_attn.astype(jnp.bfloat16), 'dp', axis=1, tiled=True)  31.2 us
  transfers between devices with their start and end apart: 17, of which 12 were waited for; matrix products, arithmetic and copies ran while one was open for 11% of the time, Pallas kernels for 0%

commit v1 on v0

--- a/solution.py
+++ b/solution.py
@@ -17,6 +17,18 @@
 masked_score = -1e30
 
 
+def collect(x, axis, dim):
+    ways, here = (lax.axis_size(axis), lax.axis_index(axis))
+    grown, reach = (x, 1)
+    while reach < ways:
+        theirs = lax.ppermute(grown, axis, [(d, d ^ reach) for d in range(ways)])
+        mine_first = jnp.concatenate([grown, theirs], axis=dim)
+        theirs_first = jnp.concatenate([theirs, grown], axis=dim)
+        grown = jnp.where(here & reach == 0, mine_first, theirs_first)
+        reach = 2 * reach
+    return grown
+
+
 def smooth_pair(values):
     squared = values * values
     bent = jnp.tanh(gelu_coef * (values + cubic_coef * squared * values))
@@ -54,7 +66,7 @@
 
 
 def rows_then_cols(local_rows, weight):
-    everyone = lax.all_gather(local_rows, "row", axis=0, tiled=True)
+    everyone = collect(local_rows, "row", 0)
     return (
         lax.psum_scatter(
             lax.dot_general(

time: 689 us -> 654 us (0.949); the launches traced: 680 us -> 653 us
  blocking collectives: 190 us -> 125 us
  waiting for transfers between devices: 328 us -> 361 us
    all_gather x4 -> x0, blocking collectives: 65.7 us -> none  [rows_then_cols(): everyone = lax.all_gather(local_rows, 'row', axis=0, tiled=True)]
    ppermute x0 -> x4, waiting for transfers between devices: none -> 32.5 us  [collect(): theirs = lax.ppermute(grown, axis, [(d, d ^ reach) for d in range(ways)])]
  transfers between devices with their start and end apart: 17 -> 21, of which waited for: 12 -> 16; matrix products, arithmetic and copies ran while one was open for 11% -> 13% of each run, Pallas kernels for 0% -> 0%
where the time goes in v1:
time: 654 us; the launch traced here: 653 us
  waiting for transfers between devices  361 us (55%)
  blocking collectives  125 us (19%)
  matrix products  90.6 us (14%)
  other arithmetic  48.4 us (7%)
  between operations  16.3 us (2%)
    reduce_scatter x4, waiting for transfers between devices, cols_then_rows(): lax.psum_scatter(jnp.dot(everyone, weight, preferred_element_type=jnp.flo...  73.7 us
    reduce_scatter x1, waiting for transfers between devices, on_device(): lax.psum_scatter(grad_up, 'dp', scatter_dimension=0, tiled=True)  70.7 us
    reduce_scatter x1, waiting for transfers between devices, on_device(): lax.psum_scatter(grad_down, 'dp', scatter_dimension=0, tiled=True)  70.5 us
    reduce_scatter x1, waiting for transfers between devices, on_device(): lax.psum_scatter(grad_attn, 'dp', scatter_dimension=1, tiled=True)  42.8 us
    psum x1, blocking collectives, on_device(): grad_norm, = lax.psum((norm_terms,), ('dp', 'row'))  42 us
    all_gather x1, blocking collectives, on_device(): lax.all_gather(w_qkv.astype(jnp.bfloat16), 'dp', axis=2, tiled=True)  32.7 us
    ppermute x4, waiting for transfers between devices, collect(): theirs = lax.ppermute(grown, axis, [(d, d ^ reach) for d in range(ways)])  32.5 us
    all_gather x1, blocking collectives, on_device(): lax.all_gather(w_attn.astype(jnp.bfloat16), 'dp', axis=1, tiled=True)  31.2 us
  transfers between devices with their start and end apart: 21, of which 16 were waited for; matrix products, arithmetic and copies ran while one was open for 13% of the time, Pallas kernels for 0%

profile of v1, /device:TPU:0, one launch (start us, length us, event | category | flops | bytes accessed | tf_op | source)
XLA Modules:
  0.0 652.8 jit_solution(8411115559810174437)
XLA Ops:
  22.5 32.7 %all_gather.24 = bf16[3,6,64,384]{3,2,1,0:T(8,128)(2,1)S(1)} all-gather(bf16[3,6,8,384]{3,2,1,0:T(8,128)(2,1)S(1)} %convert_element_type.60), channel_id=1, replica_groups=mesh['dp'=8,'row'=2,'col'=2] {'dp'}, dimensions={2}, use_global_device_ids=true | all-gather | bytes 995328 | tf_op jit(solution)/shard_map/all_gather | solution.py:182
  60.7 31.2 %all_gather.26 = bf16[6,64,384]{2,1,0:T(8,128)(2,1)S(1)} all-gather(bf16[6,8,384]{2,1,0:T(8,128)(2,1)S(1)} %convert_element_type.65), channel_id=1, replica_groups=mesh['dp'=8,'row'=2,'col'=2] {'dp'}, dimensions={1}, use_global_device_ids=true | all-gather | bytes 331776 | tf_op jit(solution)/shard_map/all_gather | solution.py:183
  108.9 15.3 %collective-permute-done.2 = bf16[512,384]{1,0:T(8,128)(2,1)S(1)} collective-permute-done((bf16[512,384]{1,0:T(8,128)(2,1)S(1)}, bf16[512,384]{1,0:T(8,128)(2,1)S(1)}, u32[]{:S(2)}, u32[]{:S(2)}) %collective-permute-start.2) | collective-permute-done | bytes 393248 | tf_op jit(solution)/shard_map/ppermute | solution.py:24
  124.2 5.9 fusion.46
  130.2 7.5 %reduce-scatter.15.cloned.1.call-done = f32[512,384]{1,0:T(8,128)} async-done(((f32[1024,384]{1,0:T(8,128)}), f32[512,384]{1,0:T(8,128)}) %reduce-scatter.15.cloned.1.call-update) | async-done | bytes 786448 | tf_op jit(solution)/shard_map/reduce_scatter | solution.py:86
  147.8 4.2 all-gather.6.cloned.1.call-done
  152.1 6.8 %collective-permute-done.1 = bf16[512,384]{1,0:T(8,128)(2,1)} collective-permute-done((bf16[512,384]{1,0:T(8,128)(2,1)}, bf16[512,384]{1,0:T(8,128)(2,1)}, u32[]{:S(2)}, u32[]{:S(2)}) %collective-permute-start.1) | collective-permute-done | bytes 393248 | tf_op jit(solution)/shard_map/ppermute | solution.py:24
  158.8 6.2 fusion.48
  165.1 14.3 %reduce-scatter.17.cloned.1.call-done = f32[512,1536]{1,0:T(8,128)} async-done(((f32[1024,1536]{1,0:T(8,128)}), f32[512,1536]{1,0:T(8,128)}) %reduce-scatter.17.cloned.1.call-update) | async-done | bytes 3145744 | tf_op jit(solution)/shard_map/reduce_scatter | solution.py:71
  179.4 5.2 multiply_convert_fusion.1
  185.2 13.7 %all-gather.12.cloned.1.call-done = bf16[1024,1536]{1,0:T(8,128)(2,1)} async-done(((bf16[512,1536]{1,0:T(8,128)(2,1)}), bf16[1024,1536]{1,0:T(8,128)(2,1)}) %all-gather.12.cloned.1.call-update) | async-done | bytes 3145744 | tf_op jit(solution)/shard_map/all_gather | solution.py:84
  198.9 5.2 fusion.87
  204.2 9.4 %all-gather.8.cloned.1.call-done = bf16[1024,1536]{1,0:T(8,128)(2,1)} async-done(((bf16[512,1536]{1,0:T(8,128)(2,1)}), bf16[1024,1536]{1,0:T(8,128)(2,1)}) %all-gather.8.cloned.1.call-update) | async-done | bytes 3145744 | tf_op jit(solution)/shard_map/all_gather | solution.py:84
  213.6 5.1 fusion.86
  218.9 24.4 %reduce-scatter.23.cloned.1.call-done = f32[512,384]{1,0:T(8,128)} async-done(((f32[1024,384]{1,0:T(8,128)}), f32[512,384]{1,0:T(8,128)}) %reduce-scatter.23.cloned.1.call-update) | async-done | bytes 786448 | tf_op jit(solution)/shard_map/reduce_scatter | solution.py:86
  249.8 21.9 %reduce-scatter.19.cloned.1.call-done = f32[512,384]{1,0:T(8,128)} async-done(((f32[1024,384]{1,0:T(8,128)}), f32[512,384]{1,0:T(8,128)}) %reduce-scatter.19.cloned.1.call-update) | async-done | bytes 786448 | tf_op jit(solution)/shard_map/reduce_scatter | solution.py:86
  274.8 10.3 %collective-permute-done.3 = bf16[512,384]{1,0:T(8,128)(2,1)S(1)} collective-permute-done((bf16[512,384]{1,0:T(8,128)(2,1)S(1)}, bf16[512,384]{1,0:T(8,128)(2,1)S(1)}, u32[]{:S(2)}, u32[]{:S(2)}) %collective-permute-start.3) | collective-permute-done | bytes 393248 | tf_op jit(solution)/shard_map/ppermute | solution.py:24
  288.1 8.9 %reduce-scatter.25.cloned.1.call-done = f32[512,384]{1,0:T(8,128)} async-done(((f32[1024,384]{1,0:T(8,128)}), f32[512,384]{1,0:T(8,128)}) %reduce-scatter.25.cloned.1.call-update) | async-done | bytes 786448 | tf_op jit(solution)/shard_map/reduce_scatter | solution.py:71
  298.4 5.3 fusion.36
  303.7 3.7 fusion.43
  307.4 13.1 %fusion.40 = bf16[512,1,6,64]{0,3,2,1:T(8,128)(2,1)} fusion(f32[6,512,512]{1,2,0:T(8,128)} %fusion.43, f32[6,512,512]{1,2,0:T(8,128)} %copy-done.1, f32[6,512]{1,0:T(8,128)S(1)} %copy-done.42, pred[512,512]{0,1:T(8,128)(4,1)} %copy-done.20, bf16[512,3,6,64]{0,3,2,1:T(8,128)(2,1)S(1)} %bitcast.158), kind=kOutput, calls=%fused_computation.30 | convolution fusion | flops 218828288 | bytes 26509312 | tf_op jit(solution)/shard_map/while/body/eval_jaxpr/hqk,khd->qhd/dot_general | solution.py:144
  320.4 11.3 %fusion.37 = bf16[512,1,6,64]{0,3,2,1:T(8,128)(2,1)} fusion(f32[6,512,512]{1,2,0:T(8,128)} %fusion.43, f32[6,512,512]{1,2,0:T(8,128)} %copy-done.1, f32[6,512]{1,0:T(8,128)S(1)} %copy-done.42, pred[512,512]{0,1:T(8,128)(4,1)} %copy-done.20, bf16[512,3,6,64]{0,3,2,1:T(8,128)(2,1)S(1)} %bitcast.159), kind=kOutput, calls=%fused_computation.29 | convolution fusion | flops 218828288 | bytes 26509312 | tf_op jit(solution)/shard_map/while/body/eval_jaxpr/hqk,qhd->khd/dot_general | solution.py:147
  336.8 5.6 fusion.47
  342.7 5.4 fusion.45
  348.3 4.4 fusion.88
  352.8 4.5 fusion.49
  357.4 42.8 %reduce-scatter.31.cloned.1.call-done = f32[6,8,384]{2,1,0:T(8,128)} async-done(((f32[6,64,384]{2,1,0:T(8,128)}), f32[6,8,384]{2,1,0:T(8,128)}) %reduce-scatter.31.cloned.1.call-update) | async-done | bytes 73744 | tf_op jit(solution)/shard_map/reduce_scatter | solution.py:236
  401.8 70.7 %reduce-scatter.33.cloned.1.call-done = f32[192,384]{1,0:T(8,128)} async-done(((f32[1536,384]{1,0:T(8,128)}), f32[192,384]{1,0:T(8,128)}) %reduce-scatter.33.cloned.1.call-update) | async-done | bytes 294928 | tf_op jit(solution)/shard_map/reduce_scatter | solution.py:237
  474.5 70.5 %reduce-scatter.35.cloned.1.call-done = f32[192,384]{1,0:T(8,128)} async-done(((f32[1536,384]{1,0:T(8,128)}), f32[192,384]{1,0:T(8,128)}) %reduce-scatter.35.cloned.1.call-update) | async-done | bytes 294928 | tf_op jit(solution)/shard_map/reduce_scatter | solution.py:238
  552.6 19.9 %reduce-scatter.27.cloned.1.call-done = f32[512,384]{1,0:T(8,128)} async-done(((f32[1024,384]{1,0:T(8,128)}), f32[512,384]{1,0:T(8,128)}) %reduce-scatter.27.cloned.1.call-update) | async-done | bytes 786448 | tf_op jit(solution)/shard_map/reduce_scatter | solution.py:86
  576.7 42.0 %psum.71 = f32[4,384]{1,0:T(4,128)S(1)} all-reduce(f32[4,384]{1,0:T(4,128)S(1)} %pad_maximum_fusion.6), channel_id=1, replica_groups=mesh['dp'=8,'row'=2,'col'=2] {'dp','row'}, use_global_device_ids=true, to_apply=%region_31.32 | all-reduce | flops 1536 | bytes 12288 | tf_op jit(solution)/shard_map/psum | solution.py:233
  622.4 19.4 %reduce-scatter.29.cloned.1.call-done = f32[3,6,8,384]{3,2,1,0:T(8,128)} async-done(((f32[3,6,64,384]{3,2,1,0:T(8,128)}), f32[3,6,8,384]{3,2,1,0:T(8,128)}) %reduce-scatter.29.cloned.1.call-update) | async-done | bytes 221200 | tf_op jit(solution)/shard_map/reduce_scatter | solution.py:235
  (199 shorter events, 89.8 us)
Async XLA Ops:
  8.0 83.9 %reduce-scatter.13.cloned.1.call-start = ((), (), s32[]{:S(2)}) async-start(), calls=%async_computation.12 | async-start | bytes 7077888 | tf_op jit(solution)/shard_map/reduce_scatter | solution.py:71
  18.7 36.6 %collective-permute-start = (bf16[512,384]{1,0:T(8,128)(2,1)S(1)}, bf16[512,384]{1,0:T(8,128)(2,1)S(1)}, u32[]{:S(2)}, u32[]{:S(2)}) collective-permute-start(bf16[512,384]{1,0:T(8,128)(2,1)S(1)} %add_convert_fusion.1), channel_id=1, source_target_pairs={{0,2},{2,0},{1,3},{3,1},{4,6},{6,4},{5,7},{7,5},{8,10},{10,8},{9,1... | collective-permute-start | bytes 1179656 | tf_op jit(solution)/shard_map/ppermute | solution.py:24
  58.9 65.3 %all-gather.10.cloned.1.call-start = ((), (), s32[]{:S(2)}) async-start(), calls=%async_computation.17 | async-start | bytes 1327104 | tf_op jit(solution)/shard_map/all_gather | solution.py:185
  60.5 77.3 %reduce-scatter.15.cloned.1.call-start = ((), (), s32[]{:S(2)}) async-start(), calls=%async_computation.13 | async-start | bytes 2359296 | tf_op jit(solution)/shard_map/reduce_scatter | solution.py:86
  107.4 44.6 %all-gather.6.cloned.1.call-start = ((), (), s32[]{:S(2)}) async-start(), calls=%async_computation.14 | async-start | bytes 1327104 | tf_op jit(solution)/shard_map/all_gather | solution.py:184
  108.2 56.9 %reduce-scatter.21.cloned.1.call-start = ((), (), s32[]{:S(2)}) async-start(), calls=%async_computation.19 | async-start | bytes 9437184 | tf_op jit(solution)/shard_map/reduce_scatter | solution.py:71
  108.3 15.9 %collective-permute-start.2 = (bf16[512,384]{1,0:T(8,128)(2,1)S(1)}, bf16[512,384]{1,0:T(8,128)(2,1)S(1)}, u32[]{:S(2)}, u32[]{:S(2)}) collective-permute-start(bf16[512,384]{1,0:T(8,128)(2,1)S(1)} %convert_element_type.70), channel_id=1, source_target_pairs={{0,2},{2,0},{1,3},{3,1},{4,6},{6,4},{5,7},{7,5},{8,10},{10,8},{9,1... | collective-permute-start | bytes 1179656 | tf_op jit(solution)/shard_map/ppermute | solution.py:24
  130.2 49.2 %reduce-scatter.17.cloned.1.call-start = ((), (), s32[]{:S(2)}) async-start(), calls=%async_computation.15 | async-start | bytes 9437184 | tf_op jit(solution)/shard_map/reduce_scatter | solution.py:71
  147.3 11.5 %collective-permute-start.1 = (bf16[512,384]{1,0:T(8,128)(2,1)}, bf16[512,384]{1,0:T(8,128)(2,1)}, u32[]{:S(2)}, u32[]{:S(2)}) collective-permute-start(bf16[512,384]{1,0:T(8,128)(2,1)} %add_convert_fusion), channel_id=1, source_target_pairs={{0,2},{2,0},{1,3},{3,1},{4,6},{6,4},{5,7},{7,5},{8,10},{10,8},{9,1... | collective-permute-start | bytes 1179656 | tf_op jit(solution)/shard_map/ppermute | solution.py:24
  165.1 33.8 %all-gather.12.cloned.1.call-start = ((), (), s32[]{:S(2)}) async-start(), calls=%async_computation.20 | async-start | bytes 4718592 | tf_op jit(solution)/shard_map/all_gather | solution.py:84
  184.6 29.0 %all-gather.8.cloned.1.call-start = ((), (), s32[]{:S(2)}) async-start(), calls=%async_computation.16 | async-start | bytes 4718592 | tf_op jit(solution)/shard_map/all_gather | solution.py:84
  185.2 58.0 %reduce-scatter.23.cloned.1.call-start = ((), (), s32[]{:S(2)}) async-start(), calls=%async_computation.21 | async-start | bytes 2359296 | tf_op jit(solution)/shard_map/reduce_scatter | solution.py:86
  204.2 67.5 %reduce-scatter.19.cloned.1.call-start = ((), (), s32[]{:S(2)}) async-start(), calls=%async_computation.18 | async-start | bytes 2359296 | tf_op jit(solution)/shard_map/reduce_scatter | solution.py:86
  218.8 78.2 %reduce-scatter.25.cloned.1.call-start = ((), (), s32[]{:S(2)}) async-start(), calls=%async_computation.22 | async-start | bytes 2359296 | tf_op jit(solution)/shard_map/reduce_scatter | solution.py:71
  274.5 10.7 %collective-permute-start.3 = (bf16[512,384]{1,0:T(8,128)(2,1)S(1)}, bf16[512,384]{1,0:T(8,128)(2,1)S(1)}, u32[]{:S(2)}, u32[]{:S(2)}) collective-permute-start(bf16[512,384]{1,0:T(8,128)(2,1)S(1)} %get-tuple-element.70), channel_id=1, source_target_pairs={{0,2},{2,0},{1,3},{3,1},{4,6},{6,4},{5,7},{7,5},{8,10},{10,8},{9,1... | collective-permute-start | bytes 1179656 | tf_op jit(solution)/shard_map/ppermute | solution.py:24
  287.8 60.5 %all-gather.14.cloned.1.call-start = ((), (), s32[]{:S(2)}) async-start(), calls=%async_computation.23 | async-start | bytes 3538944 | tf_op jit(solution)/shard_map/all_gather | solution.py:84
  334.1 66.0 %reduce-scatter.31.cloned.1.call-start = ((), (), s32[]{:S(2)}) async-start(), calls=%async_computation.26 | async-start | bytes 663552 | tf_op jit(solution)/shard_map/reduce_scatter | solution.py:236
  336.7 135.7 %reduce-scatter.33.cloned.1.call-start = ((), (), s32[]{:S(2)}) async-start(), calls=%async_computation.27 | async-start | bytes 2654208 | tf_op jit(solution)/shard_map/reduce_scatter | solution.py:237
  342.4 202.5 %reduce-scatter.35.cloned.1.call-start = ((), (), s32[]{:S(2)}) async-start(), calls=%async_computation.28 | async-start | bytes 2654208 | tf_op jit(solution)/shard_map/reduce_scatter | solution.py:238
  348.2 224.3 %reduce-scatter.27.cloned.1.call-start = ((), (), s32[]{:S(2)}) async-start(), calls=%async_computation.24 | async-start | bytes 2359296 | tf_op jit(solution)/shard_map/reduce_scatter | solution.py:86
  352.8 119.7 %copy-start.6 = (f32[2,192,384]{2,1,0:T(8,128)S(1)}, f32[2,192,384]{2,1,0:T(8,128)}, u32[]{:S(2)}) copy-start(f32[2,192,384]{2,1,0:T(8,128)} %param.22) | copy-start | bytes 1769476
  352.8 288.9 %reduce-scatter.29.cloned.1.call-start = ((), (), s32[]{:S(2)}) async-start(), calls=%async_computation.25 | async-start | bytes 1990656 | tf_op jit(solution)/shard_map/reduce_scatter | solution.py:235
  357.3 187.6 %copy-start.7 = (f32[2,192,384]{2,1,0:T(8,128)S(1)}, f32[2,192,384]{2,1,0:T(8,128)}, u32[]{:S(2)}) copy-start(f32[2,192,384]{2,1,0:T(8,128)} %param.23) | copy-start | bytes 1769476
  401.1 147.6 %copy-start.31 = (f32[6,8,384]{2,1,0:T(8,128)}, f32[6,8,384]{2,1,0:T(8,128)S(1)}, u32[]{:S(2)}) copy-start(f32[6,8,384]{2,1,0:T(8,128)S(1)} %get-tuple-element.65) | copy-start | bytes 221188
  401.1 145.9 %copy-start.32 = (f32[6,8,384]{2,1,0:T(8,128)S(1)}, f32[6,8,384]{2,1,0:T(8,128)}, u32[]{:S(2)}) copy-start(f32[6,8,384]{2,1,0:T(8,128)} %reduce-scatter.31.cloned.1.call-done) | copy-start | bytes 221188
  473.5 77.1 %copy-start.14 = (f32[192,384]{1,0:T(8,128)}, f32[192,384]{1,0:T(8,128)S(1)}, u32[]{:S(2)}) copy-start(f32[192,384]{1,0:T(8,128)S(1)} %get-tuple-element.63) | copy-start | bytes 884740
  474.4 98.1 %copy-start.36 = (f32[384]{0:T(512)S(1)}, f32[384]{0:T(512)}, u32[]{:S(2)}) copy-start(f32[384]{0:T(512)} %copy-done.35) | copy-start | bytes 4612
  474.5 98.1 %copy-start.38 = (f32[512,1]{0,1:T(1,128)S(1)}, f32[512,1]{0,1:T(1,128)}, u32[]{:S(2)}) copy-start(f32[512,1]{0,1:T(1,128)} %copy-done.37) | copy-start | bytes 6148
  546.1 72.6 %copy-start.34 = (f32[2,4,384]{2,1,0:T(4,128)S(1)}, f32[2,4,384]{2,1,0:T(4,128)}, u32[]{:S(2)}) copy-start(f32[2,4,384]{2,1,0:T(4,128)} %param.19) | copy-start | bytes 36868
  546.1 73.3 %copy-start.39 = (f32[4,384]{1,0:T(4,128)S(1)}, f32[4,384]{1,0:T(4,128)}, u32[]{:S(2)}) copy-start(f32[4,384]{1,0:T(4,128)} %param.14) | copy-start | bytes 18436
  547.0 73.0 %copy-start.3 = (f32[512,384]{1,0:T(8,128)S(1)}, f32[512,384]{1,0:T(8,128)}, u32[]{:S(2)}) copy-start(f32[512,384]{1,0:T(8,128)} %get-tuple-element.71) | copy-start | bytes 2359300
  550.6 91.1 %copy-start.9 = (f32[2,3,6,8,384]{4,3,2,1,0:T(8,128)S(1)}, f32[2,3,6,8,384]{4,3,2,1,0:T(8,128)}, u32[]{:S(2)}) copy-start(f32[2,3,6,8,384]{4,3,2,1,0:T(8,128)} %param.20) | copy-start | bytes 1327108
  (35 other events, 420.8 us)
Sparse Core Ops, SparseCore 0:
  59.0 12.7 reduce-scatter.12
  107.6 30.1 reduce-scatter.14
  140.1 14.1 reduce-scatter.20
  165.2 14.1 reduce-scatter.16
  184.7 14.1 all-gather.11
  200.3 13.2 all-gather.7
  215.9 27.3 reduce-scatter.22
  245.5 26.1 reduce-scatter.18
  287.9 9.0 reduce-scatter.24
  334.2 12.2 all-gather.13
Sparse Core Ops, SparseCore 1:
  62.1 41.5 all-gather.9
  110.7 41.3 all-gather.5
  338.5 61.6 reduce-scatter.30
  403.7 68.7 reduce-scatter.32
  476.0 68.9 reduce-scatter.34
  547.2 25.3 reduce-scatter.26
  575.9 65.8 reduce-scatter.28
